TPU v7x, 32 devices: a whole 2x2x4 slice. The times are simulated.
32 devices in a mesh: prow: 4 (over y, x), pcol: 8 (over z, core).
Axes of the slice: x: 2, y: 2, z: 4, core: 2. Of those that a mesh axis runs over, the one named last changes fastest.
Arguments:
- rhs: bfloat16 [3, 8, 512, 128], P(None, 'pcol', 'prow'), may hold values from -6 to 6
- inverse_diagonal_blocks: bfloat16 [3, 8, 512, 512], P(None, 'pcol'), may hold values from -1 to 2, as said below
- offdiagonal_blocks: bfloat16 [2, 8, 4, 512, 512], P(None, 'pcol', 'prow'), may hold values from -0.09375 to 0.09375
- targets: int32 [2, 8, 4], P(None, 'pcol'), may hold values from 0 to 15, as said below
Outputs:
- solution: bfloat16 [3, 8, 512, 128], P(None, 'pcol', 'prow')
Inputs may be any that keep to these rules, and one draw needn't show every extreme that they name: For a supernode of level l the 4 entries of targets[l] are distinct and lie between l * 8 and (2) * 8 - 1, so they name supernodes of later levels only. Each block of inverse_diagonal_blocks is lower triangular.
All inputs are finite; a program needn't handle non-finite values.
Results may differ from a plain program's by a relative error of at most 0.014.
Values may be sent and summed in bfloat16 or wider, within the bound.
No kernel may reach another device: no remote copies, remote signals or barrier semaphores. Data moves between devices by JAX's collectives and lax.ppermute only.
A program may use at most 64 MiB of HBM per device.

v0:
```python
import jax
import jax.numpy as jnp
from jax import lax
from jax.sharding import PartitionSpec as P


def local(rhs, inverse_diagonal_blocks, offdiagonal_blocks, targets):
    levels = rhs.shape[0]
    per_group = rhs.shape[1]
    part_rows = rhs.shape[2]
    vector_count = rhs.shape[3]
    per_device = offdiagonal_blocks.shape[2]
    row_count = lax.axis_size("prow")
    level_size = per_group * lax.axis_size("pcol")
    upper_count = levels - 1
    row_index = lax.axis_index("prow")
    gathered_updates = jnp.zeros(
        (upper_count, row_count, level_size, part_rows, vector_count), jnp.float32
    )
    outputs = []
    for present_level in range(levels):
        remaining_rhs = rhs[present_level].astype(jnp.float32)
        if present_level > 0:
            due_block = gathered_updates[present_level - 1]
            reduced_once = lax.psum_scatter(
                due_block.astype(jnp.bfloat16), "pcol", scatter_dimension=1, tiled=True
            )
            arrived = lax.psum_scatter(
                reduced_once, "prow", scatter_dimension=0, tiled=True
            ).astype(jnp.float32)[0]
            remaining_rhs = remaining_rhs - arrived
        whole_block = lax.all_gather(remaining_rhs, "prow", axis=1, tiled=True)
        finished_unknowns = jnp.einsum(
            "rqe,rei->rqi",
            inverse_diagonal_blocks[present_level].astype(jnp.float32),
            whole_block,
            precision=lax.Precision.HIGHEST,
        ).astype(jnp.bfloat16)
        supernode_rows = lax.dynamic_slice_in_dim(
            finished_unknowns, row_index * part_rows, part_rows, 1
        )
        outputs.append(supernode_rows)
        if present_level < upper_count:
            products = jnp.einsum(
                "wsiq,wqm->wsim",
                offdiagonal_blocks[present_level],
                finished_unknowns,
                preferred_element_type=jnp.float32,
            )
            chosen = lax.dynamic_slice_in_dim(
                targets[present_level], row_index * per_device, per_device, 1
            )
            chosen = chosen.reshape(per_group * per_device)
            level_ids = chosen // level_size
            node_ids = chosen % level_size
            moved_rows = products.reshape(
                per_group * per_device, row_count, part_rows, vector_count
            )
            gathered_updates = gathered_updates.at[level_ids, :, node_ids].add(moved_rows)
    return jnp.stack(outputs)


def solution(mesh):
    in_specs = (
        P(None, "pcol", "prow", None),
        P(None, "pcol", None, None),
        P(None, "pcol", "prow", None, None),
        P(None, "pcol", None),
    )
    out_specs = P(None, "pcol", "prow", None)
    return jax.shard_map(local, mesh=mesh, in_specs=in_specs, out_specs=out_specs, check_vma=False)
```

profile of v0, /device:TPU:0, one launch (start us, length us, event | category | flops | bytes accessed | tf_op | source)
XLA Modules:
  0.0 184.7 jit_solution(10603757281627997184)
XLA Ops:
  6.5 0.7 fusion.22
  7.2 0.6 constant_dynamic-slice_fusion
  13.0 0.8 fusion.21
  13.8 10.5 %all-gather = f32[1,1,512,128]{3,2,1,0:T(8,128)S(1)} all-gather(f32[1,1,128,128]{3,2,1,0:T(8,128)S(1)} %get-tuple-element.35), channel_id=2, replica_groups=mesh['prow'=4,'pcol'=8] {'prow'}, dimensions={2}, use_global_device_ids=true | all-gather | bytes 327680 | tf_op jit(solution)/shard_map/all_gather | solution.py:32
  24.3 1.3 fusion.20
  25.7 1.6 convolution_convert_fusion.1
  27.4 1.4 and_reduce_fusion
  28.7 0.5 broadcast_in_dim.2
  29.2 0.9 fusion.1
  30.2 1.9 %copy-done = f32[2,4,8,128,128]{3,4,1,2,0:T(8,128)} copy-done((f32[2,4,8,128,128]{3,4,1,2,0:T(8,128)}, f32[2,4,8,128,128]{3,4,1,2,0:T(8,128)S(1)}, u32[]{:S(2)}) %copy-start) | copy-done | bytes 4194328
  32.1 1.1 fusion.5
  33.3 33.0 %reduce-scatter.15.cloned.1.call-done = bf16[4,1,128,128]{2,3,0,1:T(8,128)(2,1)} async-done(((bf16[4,8,128,128]{2,3,0,1:T(8,128)(2,1)}), bf16[4,1,128,128]{2,3,0,1:T(8,128)(2,1)}) %reduce-scatter.15.cloned.1.call-update) | async-done | bytes 131088 | tf_op jit(solution)/shard_map/reduce_scatter | solution.py:25
  66.5 24.9 %reduce-scatter.19.cloned.1.call-done = bf16[1,1,128,128]{2,3,0,1:T(8,128)(2,1)} async-done(((bf16[4,1,128,128]{2,3,0,1:T(8,128)(2,1)}), bf16[1,1,128,128]{2,3,0,1:T(8,128)(2,1)}) %reduce-scatter.19.cloned.1.call-update) | async-done | bytes 32784
  91.4 0.8 convert_subtract_fusion.1
  92.2 10.0 %all-gather.1 = f32[1,1,512,128]{2,3,0,1:T(8,128)S(1)} all-gather(f32[1,1,128,128]{2,3,0,1:T(8,128)S(1)} %convert_subtract_fusion.1), channel_id=3, replica_groups=mesh['prow'=4,'pcol'=8] {'prow'}, dimensions={2}, use_global_device_ids=true | all-gather | bytes 327680 | tf_op jit(solution)/shard_map/all_gather | solution.py:32
  102.2 0.7 convolution_convert_fusion
  102.9 2.6 %fusion.4 = f32[2,4,8,128,128]{3,4,1,2,0:T(8,128)} fusion(f32[2,4,8,128,128]{3,4,1,2,0:T(8,128)} %copy-done, s32[]{:T(128)} %bitcast.16, s32[]{:T(128)} %bitcast.17, bf16[4,128,512]{2,1,0:T(8,128)(2,1)S(1)} %bitcast.81, bf16[128,512]{1,0:T(8,128)(2,1)S(1)} %convolution_convert_fusion, pred[]{:T(512)} %get-tuple-element.29), kind=kOutput, calls=%fused_computation.8 | convolution fusion | flops 67239936 | bytes 1181184 | tf_op jit(solution)/shard_map/wsiq,wqm->wsim/dot_general | solution.py:44
  105.5 2.7 %fusion.6 = bf16[4,8,128,128]{2,3,0,1:T(8,128)(2,1)} fusion(f32[2,4,8,128,128]{3,4,1,2,0:T(8,128)} %fusion.4), kind=kLoop, calls=%fused_computation.12 | loop fusion | bytes 2097152 | tf_op jit(solution)/shard_map/convert_element_type | solution.py:26
  108.2 32.7 %reduce-scatter.17.cloned.1.call-done = bf16[4,1,128,128]{2,3,0,1:T(8,128)(2,1)} async-done(((bf16[4,8,128,128]{2,3,0,1:T(8,128)(2,1)}), bf16[4,1,128,128]{2,3,0,1:T(8,128)(2,1)}) %reduce-scatter.17.cloned.1.call-update) | async-done | bytes 131088 | tf_op jit(solution)/shard_map/reduce_scatter | solution.py:25
  141.2 24.6 %reduce-scatter.21.cloned.1.call-done = bf16[1,1,128,128]{2,3,0,1:T(8,128)(2,1)} async-done(((bf16[4,1,128,128]{2,3,0,1:T(8,128)(2,1)}), bf16[1,1,128,128]{2,3,0,1:T(8,128)(2,1)}) %reduce-scatter.21.cloned.1.call-update) | async-done | bytes 32784
  165.9 0.8 convert_subtract_fusion
  166.7 10.0 %all-gather.2 = f32[1,1,512,128]{2,3,0,1:T(8,128)S(1)} all-gather(f32[1,1,128,128]{2,3,0,1:T(8,128)S(1)} %convert_subtract_fusion), channel_id=4, replica_groups=mesh['prow'=4,'pcol'=8] {'prow'}, dimensions={2}, use_global_device_ids=true | all-gather | bytes 327680 | tf_op jit(solution)/shard_map/all_gather | solution.py:32
  176.7 0.7 fusion.7
  177.4 0.8 copy.18
  (20 shorter events, 0.7 us)
Async XLA Ops:
  6.5 59.8 %reduce-scatter.15.cloned.1.call-start = ((), (), s32[]{:S(2)}) async-start(), calls=%async_computation.4 | async-start | bytes 1179648 | tf_op jit(solution)/shard_map/reduce_scatter | solution.py:25
  28.7 73.4 %copy-start.1 = (bf16[3,1,512,512]{3,2,1,0:T(8,128)(2,1)S(1)}, bf16[3,1,512,512]{3,2,1,0:T(8,128)(2,1)}, u32[]{:S(2)}) copy-start(bf16[3,1,512,512]{3,2,1,0:T(8,128)(2,1)} %param.9) | copy-start | bytes 4718596
  30.2 1.9 %copy-start = (f32[2,4,8,128,128]{3,4,1,2,0:T(8,128)}, f32[2,4,8,128,128]{3,4,1,2,0:T(8,128)S(1)}, u32[]{:S(2)}) copy-start(f32[2,4,8,128,128]{3,4,1,2,0:T(8,128)S(1)} %fusion.1) | copy-start | bytes 12582916
  33.3 58.1 %reduce-scatter.19.cloned.1.call-start = ((), (), s32[]{:S(2)}) async-start(), calls=%async_computation.6 | async-start | bytes 163840
  66.4 74.6 %reduce-scatter.17.cloned.1.call-start = ((), (), s32[]{:S(2)}) async-start(), calls=%async_computation.5 | async-start | bytes 1179648 | tf_op jit(solution)/shard_map/reduce_scatter | solution.py:25
  108.2 57.7 %reduce-scatter.21.cloned.1.call-start = ((), (), s32[]{:S(2)}) async-start(), calls=%async_computation.7 | async-start | bytes 163840
Sparse Core Ops, SparseCore 0:
  33.4 32.8 reduce-scatter.14
  69.1 22.3 reduce-scatter.18
  108.3 32.5 reduce-scatter.16
  143.5 22.3 reduce-scatter.20
where the time goes:
time: 185 us
  waiting for transfers between devices  115 us (62%)
  blocking collectives  30.4 us (16%)
  between operations  18.4 us (10%)
  local copies, waits for them, and re-layouts  10.1 us (5%)
  matrix products  6.49 us (4%)
  other arithmetic  3.72 us (2%)
    reduce_scatter x2, waiting for transfers between devices, local(): lax.psum_scatter(due_block.astype(jnp.bfloat16), 'pcol', scatter_dimensio...  65.7 us
    unnamed x6, waiting for transfers between devices  49.6 us
    all_gather x3, blocking collectives, local(): whole_block = lax.all_gather(remaining_rhs, 'prow', axis=1, tiled=True)  30.4 us
    convert_element_type x2, local copies, waits for them, and re-layouts, local(): due_block.astype(jnp.bfloat16)  3.85 us
  transfers between devices with their start and end apart: 4, of which 4 were waited for; matrix products, arithmetic and copies ran while one was open for 0% of the time, Pallas kernels for 0%

commit v1 on v0

--- a/solution.py
+++ b/solution.py
@@ -2,6 +2,19 @@
 import jax.numpy as jnp
 from jax import lax
 from jax.sharding import PartitionSpec as P
+
+
+def collect(shard, axis, dim):
+    ways = lax.axis_size(axis)
+    up = [(d, (d + 1) % ways) for d in range(ways)]
+    down = [(d, (d - 1) % ways) for d in range(ways)]
+    earlier, later = ([shard], [shard])
+    for _ in range(ways // 2):
+        earlier.append(lax.ppermute(earlier[-1], axis, up))
+    for _ in range((ways - 1) // 2):
+        later.append(lax.ppermute(later[-1], axis, down))
+    line = jnp.concatenate([*earlier[::-1], *later[1:]], axis=dim)
+    return jnp.roll(line, (lax.axis_index(axis) - ways // 2) * shard.shape[dim], axis=dim)
 
 
 def local(rhs, inverse_diagonal_blocks, offdiagonal_blocks, targets):
@@ -29,7 +42,7 @@
                 reduced_once, "prow", scatter_dimension=0, tiled=True
             ).astype(jnp.float32)[0]
             remaining_rhs = remaining_rhs - arrived
-        whole_block = lax.all_gather(remaining_rhs, "prow", axis=1, tiled=True)
+        whole_block = collect(remaining_rhs, "prow", 1)
         finished_unknowns = jnp.einsum(
             "rqe,rei->rqi",
             inverse_diagonal_blocks[present_level].astype(jnp.float32),

time: 185 us -> 184 us (level)
  blocking collectives: 30.4 us -> 0 us
  waiting for transfers between devices: 115 us -> 132 us
  starting transfers between devices: 0.12 us -> 12.6 us
    all_gather x3 -> x0, blocking collectives: 30.4 us -> none  [local(): whole_block = lax.all_gather(remaining_rhs, 'prow', axis=1, tiled=True)]
    ppermute x0 -> x9, waiting for transfers between devices: none -> 16.1 us  [the longest x6 16.1 us: collect(): earlier.append(lax.ppermute(earlier[-1], axis, up))]
    ppermute x0 -> x9, starting transfers between devices: none -> 12.5 us  [the longest x6 8.56 us: collect(): earlier.append(lax.ppermute(earlier[-1], axis, up))]
  transfers between devices with their start and end apart: 4 -> 13, of which waited for: 4 -> 9; matrix products, arithmetic and copies ran while one was open for 0% -> 2% of each run, Pallas kernels for 0% -> 0%
where the time goes in v1:
time: 184 us
  waiting for transfers between devices  132 us (72%)
  between operations  18.4 us (10%)
  starting transfers between devices  12.6 us (7%)
  local copies, waits for them, and re-layouts  10 us (5%)
  matrix products  6.93 us (4%)
  other arithmetic  3.71 us (2%)
    reduce_scatter x2, waiting for transfers between devices, local(): lax.psum_scatter(due_block.astype(jnp.bfloat16), 'pcol', scatter_dimensio...  66.1 us
    unnamed x6, waiting for transfers between devices  49.9 us
    ppermute x6, waiting for transfers between devices, collect(): earlier.append(lax.ppermute(earlier[-1], axis, up))  16.1 us
    ppermute x6, starting transfers between devices, collect(): earlier.append(lax.ppermute(earlier[-1], axis, up))  8.56 us
    ppermute x3, starting transfers between devices, collect(): later.append(lax.ppermute(later[-1], axis, down))  3.96 us
    convert_element_type x2, local copies, waits for them, and re-layouts, local(): due_block.astype(jnp.bfloat16)  3.84 us
  transfers between devices with their start and end apart: 13, of which 9 were waited for; matrix products, arithmetic and copies ran while one was open for 2% of the time, Pallas kernels for 0%

profile of v1, /device:TPU:0, one launch (start us, length us, event | category | flops | bytes accessed | tf_op | source)
XLA Modules:
  0.0 183.8 jit_solution(11204651528277809260)
XLA Ops:
  7.3 3.0 %collective-permute-start = (f32[1,128,128]{2,1,0:T(8,128)S(1)}, f32[1,128,128]{2,1,0:T(8,128)S(1)}, u32[]{:S(2)}, u32[]{:S(2)}) collective-permute-start(f32[1,128,128]{2,1,0:T(8,128)S(1)} %get-tuple-element.36), channel_id=1, source_target_pairs={{0,8},{8,16},{16,24},{24,0},{1,9},{9,17},{17,25},{25,1},{2,10},{10... | collective-permute-start | bytes 196616 | tf_op jit(solution)/shard_map/ppermute | solution.py:13
  10.4 1.0 collective-permute-start.2
  11.4 1.3 fusion.53
  19.3 1.0 collective-permute-start.1
  20.3 1.4 and_reduce_fusion
  21.7 2.8 %collective-permute-done.1 = f32[1,128,128]{2,1,0:T(8,128)S(1)} collective-permute-done((f32[1,128,128]{2,1,0:T(8,128)S(1)}, f32[1,128,128]{2,1,0:T(8,128)S(1)}, u32[]{:S(2)}, u32[]{:S(2)}) %collective-permute-start.1) | collective-permute-done | bytes 65568 | tf_op jit(solution)/shard_map/ppermute | solution.py:13
  24.5 2.2 %convolution_convert_fusion.1 = bf16[128,512]{1,0:T(8,128)(2,1)S(1)} fusion(bf16[3,1,512,512]{3,2,1,0:T(8,128)(2,1)} %param.11, s32[]{:T(128)S(6)} %select_n.64, f32[1,128,128]{2,1,0:T(8,128)S(1)} %collective-permute-done.1, f32[1,128,128]{2,1,0:T(8,128)S(1)} %collective-permute-done, f32[1,128,128]{2,1,0:T(8,128)S(1)} %get-tuple-element.36, ...), kind=kOutput, calls=%fused_computation.10 | convolution fusion | flops 403177472 | bytes 917508 | tf_op jit(solution)/shard_map/rqe,rei->rqi/dot_general | solution.py:46
  27.2 0.9 fusion.1
  28.2 1.9 %copy-done = f32[2,4,8,128,128]{3,4,1,2,0:T(8,128)} copy-done((f32[2,4,8,128,128]{3,4,1,2,0:T(8,128)}, f32[2,4,8,128,128]{3,4,1,2,0:T(8,128)S(1)}, u32[]{:S(2)}) %copy-start) | copy-done | bytes 4194328
  30.1 1.1 fusion.5
  31.3 33.4 %reduce-scatter.15.cloned.1.call-done = bf16[4,1,128,128]{2,3,0,1:T(8,128)(2,1)} async-done(((bf16[4,8,128,128]{2,3,0,1:T(8,128)(2,1)}), bf16[4,1,128,128]{2,3,0,1:T(8,128)(2,1)}) %reduce-scatter.15.cloned.1.call-update) | async-done | bytes 131088 | tf_op jit(solution)/shard_map/reduce_scatter | solution.py:38
  64.9 25.0 %reduce-scatter.19.cloned.1.call-done = bf16[1,1,128,128]{2,3,0,1:T(8,128)(2,1)} async-done(((bf16[4,1,128,128]{2,3,0,1:T(8,128)(2,1)}), bf16[1,1,128,128]{2,3,0,1:T(8,128)(2,1)}) %reduce-scatter.19.cloned.1.call-update) | async-done | bytes 32784
  90.7 1.5 collective-permute-start.3
  92.2 1.5 collective-permute-start.5
  93.6 2.2 %collective-permute-done.3 = f32[1,128,128]{1,2,0:T(8,128)S(1)} collective-permute-done((f32[1,128,128]{1,2,0:T(8,128)S(1)}, f32[1,128,128]{1,2,0:T(8,128)S(1)}, u32[]{:S(2)}, u32[]{:S(2)}) %collective-permute-start.3) | collective-permute-done | bytes 65568 | tf_op jit(solution)/shard_map/ppermute | solution.py:13
  96.6 4.4 %collective-permute-done.4 = f32[1,128,128]{1,2,0:T(8,128)S(1)} collective-permute-done((f32[1,128,128]{1,2,0:T(8,128)S(1)}, f32[1,128,128]{1,2,0:T(8,128)S(1)}, u32[]{:S(2)}, u32[]{:S(2)}) %collective-permute-start.4) | collective-permute-done | bytes 65568 | tf_op jit(solution)/shard_map/ppermute | solution.py:13
  101.7 2.5 %fusion.4 = f32[2,4,8,128,128]{3,4,1,2,0:T(8,128)} fusion(f32[2,4,8,128,128]{3,4,1,2,0:T(8,128)} %copy-done, s32[]{:T(128)} %bitcast.20, s32[]{:T(128)} %bitcast.21, bf16[4,128,512]{2,1,0:T(8,128)(2,1)S(1)} %bitcast.90, bf16[128,512]{1,0:T(8,128)(2,1)S(1)} %convolution_convert_fusion, pred[]{:T(512)} %get-tuple-element.30), kind=kOutput, calls=%fused_computation.8 | convolution fusion | flops 67239936 | bytes 1181184 | tf_op jit(solution)/shard_map/wsiq,wqm->wsim/dot_general | solution.py:57
  104.2 2.7 %fusion.6 = bf16[4,8,128,128]{2,3,0,1:T(8,128)(2,1)} fusion(f32[2,4,8,128,128]{3,4,1,2,0:T(8,128)} %fusion.4), kind=kLoop, calls=%fused_computation.12 | loop fusion | bytes 2097152 | tf_op jit(solution)/shard_map/convert_element_type | solution.py:39
  107.0 32.7 %reduce-scatter.17.cloned.1.call-done = bf16[4,1,128,128]{2,3,0,1:T(8,128)(2,1)} async-done(((bf16[4,8,128,128]{2,3,0,1:T(8,128)(2,1)}), bf16[4,1,128,128]{2,3,0,1:T(8,128)(2,1)}) %reduce-scatter.17.cloned.1.call-update) | async-done | bytes 131088 | tf_op jit(solution)/shard_map/reduce_scatter | solution.py:38
  139.8 24.9 %reduce-scatter.21.cloned.1.call-done = bf16[1,1,128,128]{2,3,0,1:T(8,128)(2,1)} async-done(((bf16[4,1,128,128]{2,3,0,1:T(8,128)(2,1)}), bf16[1,1,128,128]{2,3,0,1:T(8,128)(2,1)}) %reduce-scatter.21.cloned.1.call-update) | async-done | bytes 32784
  165.4 1.5 collective-permute-start.6
  166.9 1.5 collective-permute-start.8
  168.4 2.2 %collective-permute-done.6 = f32[1,128,128]{1,2,0:T(8,128)S(1)} collective-permute-done((f32[1,128,128]{1,2,0:T(8,128)S(1)}, f32[1,128,128]{1,2,0:T(8,128)S(1)}, u32[]{:S(2)}, u32[]{:S(2)}) %collective-permute-start.6) | collective-permute-done | bytes 65568 | tf_op jit(solution)/shard_map/ppermute | solution.py:13
  171.4 4.4 %collective-permute-done.7 = f32[1,128,128]{1,2,0:T(8,128)S(1)} collective-permute-done((f32[1,128,128]{1,2,0:T(8,128)S(1)}, f32[1,128,128]{1,2,0:T(8,128)S(1)}, u32[]{:S(2)}, u32[]{:S(2)}) %collective-permute-start.7) | collective-permute-done | bytes 65568 | tf_op jit(solution)/shard_map/ppermute | solution.py:13
  (34 shorter events, 8.3 us)
Async XLA Ops:
  6.5 58.2 %reduce-scatter.15.cloned.1.call-start = ((), (), s32[]{:S(2)}) async-start(), calls=%async_computation.4 | async-start | bytes 1179648 | tf_op jit(solution)/shard_map/reduce_scatter | solution.py:38
  7.3 12.0 %collective-permute-start = (f32[1,128,128]{2,1,0:T(8,128)S(1)}, f32[1,128,128]{2,1,0:T(8,128)S(1)}, u32[]{:S(2)}, u32[]{:S(2)}) collective-permute-start(f32[1,128,128]{2,1,0:T(8,128)S(1)} %get-tuple-element.36), channel_id=1, source_target_pairs={{0,8},{8,16},{16,24},{24,0},{1,9},{9,17},{17,25},{25,1},{2,10},{10... | collective-permute-start | bytes 196616 | tf_op jit(solution)/shard_map/ppermute | solution.py:13
  10.4 11.3 %collective-permute-start.2 = (f32[1,128,128]{2,1,0:T(8,128)S(1)}, f32[1,128,128]{2,1,0:T(8,128)S(1)}, u32[]{:S(2)}, u32[]{:S(2)}) collective-permute-start(f32[1,128,128]{2,1,0:T(8,128)S(1)} %get-tuple-element.36), channel_id=1, source_target_pairs={{0,24},{8,0},{16,8},{24,16},{1,25},{9,1},{17,9},{25,17},{2,26},{10... | collective-permute-start | bytes 196616 | tf_op jit(solution)/shard_map/ppermute | solution.py:15
  19.3 5.2 %collective-permute-start.1 = (f32[1,128,128]{2,1,0:T(8,128)S(1)}, f32[1,128,128]{2,1,0:T(8,128)S(1)}, u32[]{:S(2)}, u32[]{:S(2)}) collective-permute-start(f32[1,128,128]{2,1,0:T(8,128)S(1)} %collective-permute-done), channel_id=1, source_target_pairs={{0,8},{8,16},{16,24},{24,0},{1,9},{9,17},{17,25},{25,1},{2,10},{10... | collective-permute-start | bytes 196616 | tf_op jit(solution)/shard_map/ppermute | solution.py:13
  26.7 74.3 %copy-start.1 = (bf16[3,1,512,512]{3,2,1,0:T(8,128)(2,1)S(1)}, bf16[3,1,512,512]{3,2,1,0:T(8,128)(2,1)}, u32[]{:S(2)}) copy-start(bf16[3,1,512,512]{3,2,1,0:T(8,128)(2,1)} %param.11) | copy-start | bytes 4718596
  28.2 1.9 %copy-start = (f32[2,4,8,128,128]{3,4,1,2,0:T(8,128)}, f32[2,4,8,128,128]{3,4,1,2,0:T(8,128)S(1)}, u32[]{:S(2)}) copy-start(f32[2,4,8,128,128]{3,4,1,2,0:T(8,128)S(1)} %fusion.1) | copy-start | bytes 12582916
  31.3 58.6 %reduce-scatter.19.cloned.1.call-start = ((), (), s32[]{:S(2)}) async-start(), calls=%async_computation.6 | async-start | bytes 163840
  64.7 74.9 %reduce-scatter.17.cloned.1.call-start = ((), (), s32[]{:S(2)}) async-start(), calls=%async_computation.5 | async-start | bytes 1179648 | tf_op jit(solution)/shard_map/reduce_scatter | solution.py:38
  90.7 5.2 %collective-permute-start.3 = (f32[1,128,128]{1,2,0:T(8,128)S(1)}, f32[1,128,128]{1,2,0:T(8,128)S(1)}, u32[]{:S(2)}, u32[]{:S(2)}) collective-permute-start(f32[1,128,128]{1,2,0:T(8,128)S(1)} %subtract_bitcast_fusion.1), channel_id=1, source_target_pairs={{0,8},{8,16},{16,24},{24,0},{1,9},{9,17},{17,25},{25,1},{2,10},{10... | collective-permute-start | bytes 196616 | tf_op jit(solution)/shard_map/ppermute | solution.py:13
  92.2 4.5 %collective-permute-start.5 = (f32[1,128,128]{1,2,0:T(8,128)S(1)}, f32[1,128,128]{1,2,0:T(8,128)S(1)}, u32[]{:S(2)}, u32[]{:S(2)}) collective-permute-start(f32[1,128,128]{1,2,0:T(8,128)S(1)} %subtract_bitcast_fusion.1), channel_id=1, source_target_pairs={{0,24},{8,0},{16,8},{24,16},{1,25},{9,1},{17,9},{25,17},{2,26},{10... | collective-permute-start | bytes 196616 | tf_op jit(solution)/shard_map/ppermute | solution.py:15
  95.9 5.2 %collective-permute-start.4 = (f32[1,128,128]{1,2,0:T(8,128)S(1)}, f32[1,128,128]{1,2,0:T(8,128)S(1)}, u32[]{:S(2)}, u32[]{:S(2)}) collective-permute-start(f32[1,128,128]{1,2,0:T(8,128)S(1)} %collective-permute-done.3), channel_id=1, source_target_pairs={{0,8},{8,16},{16,24},{24,0},{1,9},{9,17},{17,25},{25,1},{2,10},{10... | collective-permute-start | bytes 196616 | tf_op jit(solution)/shard_map/ppermute | solution.py:13
  106.9 57.7 %reduce-scatter.21.cloned.1.call-start = ((), (), s32[]{:S(2)}) async-start(), calls=%async_computation.7 | async-start | bytes 163840
  165.4 5.2 %collective-permute-start.6 = (f32[1,128,128]{1,2,0:T(8,128)S(1)}, f32[1,128,128]{1,2,0:T(8,128)S(1)}, u32[]{:S(2)}, u32[]{:S(2)}) collective-permute-start(f32[1,128,128]{1,2,0:T(8,128)S(1)} %subtract_bitcast_fusion), channel_id=1, source_target_pairs={{0,8},{8,16},{16,24},{24,0},{1,9},{9,17},{17,25},{25,1},{2,10},{10... | collective-permute-start | bytes 196616 | tf_op jit(solution)/shard_map/ppermute | solution.py:13
  166.9 4.5 %collective-permute-start.8 = (f32[1,128,128]{1,2,0:T(8,128)S(1)}, f32[1,128,128]{1,2,0:T(8,128)S(1)}, u32[]{:S(2)}, u32[]{:S(2)}) collective-permute-start(f32[1,128,128]{1,2,0:T(8,128)S(1)} %subtract_bitcast_fusion), channel_id=1, source_target_pairs={{0,24},{8,0},{16,8},{24,16},{1,25},{9,1},{17,9},{25,17},{2,26},{10... | collective-permute-start | bytes 196616 | tf_op jit(solution)/shard_map/ppermute | solution.py:15
  170.6 5.2 %collective-permute-start.7 = (f32[1,128,128]{1,2,0:T(8,128)S(1)}, f32[1,128,128]{1,2,0:T(8,128)S(1)}, u32[]{:S(2)}, u32[]{:S(2)}) collective-permute-start(f32[1,128,128]{1,2,0:T(8,128)S(1)} %collective-permute-done.6), channel_id=1, source_target_pairs={{0,8},{8,16},{16,24},{24,0},{1,9},{9,17},{17,25},{25,1},{2,10},{10... | collective-permute-start | bytes 196616 | tf_op jit(solution)/shard_map/ppermute | solution.py:13
Sparse Core Ops, SparseCore 0:
  31.4 33.2 reduce-scatter.14
  67.4 22.3 reduce-scatter.18
  107.1 32.5 reduce-scatter.16
  142.3 22.3 reduce-scatter.20
